TPU v7x, 32 devices: a whole 2x2x4 slice. The times are simulated.
32 devices in a mesh: ctx: 8 (over y, x, core), kvh: 4 (over z).
Axes of the slice: x: 2, y: 2, z: 4, core: 2. Of those that a mesh axis runs over, the one named last changes fastest.
Arguments:
- query_heads: bfloat16 [16384, 4096], P('ctx', 'kvh'), may hold values from -8 to 8
- key_heads: bfloat16 [16384, 1024], P('ctx', 'kvh'), may hold values from -4.5 to 4.5
- value_head_rows: bfloat16 [16384, 1024], P('ctx', 'kvh'), may hold values from -6 to 6
- out_weight: bfloat16 [4096, 4096], P('kvh'), may hold values from -0.09375 to 0.09375
- piece_lengths: int32 [16], replicated, may hold values from 1 to 4096, 16384 in all
- block_order: int32 [128], replicated, may hold values from 0 to 127, as said below
Outputs:
- mixed: bfloat16 [16384, 4096], P(('ctx', 'kvh'))
Inputs may be any that keep to these rules, and one draw needn't show every extreme that they name: `block_order`: a permutation of the blocks; slot d * 16 + s * 2 + j with 0 <= j < 2 holds a block of the contiguous range s * 16 to (s + 1) * 16 - 1. `piece_lengths`: they sum to 16384.
All inputs are finite; a program needn't handle non-finite values.
Results may differ from a plain program's by a relative error of at most 0.013.
Values may be sent and summed in bfloat16 or wider, within the bound.
A program may use at most 128 MiB of HBM per device.

v0:
```python
import jax
import jax.numpy as jnp
from jax import lax
from jax.sharding import PartitionSpec as P

HEAD_SIZE = 128
BLK = 128
MOST = 4096


def piece_starts(positions, piece_lengths):
    piece_ends = jnp.cumsum(piece_lengths)
    chosen = jnp.where(piece_ends[None, :] <= positions[:, None], piece_lengths[None, :], 0)
    return jnp.sum(chosen, axis=1)


def attend(query_block, key_window, value_window, query_pos, key_pos, query_start):
    groups = key_window.shape[1] // HEAD_SIZE
    per_group = query_block.shape[1] // key_window.shape[1]
    query_four = query_block.reshape(query_block.shape[0], groups, per_group, HEAD_SIZE)
    key_three = key_window.reshape(-1, groups, HEAD_SIZE)
    value_three = value_window.reshape(-1, groups, HEAD_SIZE)
    scores = jnp.einsum(
        "qgjd,kgd->gjqk", query_four, key_three, preferred_element_type=jnp.float32
    ) * (1.0 / HEAD_SIZE**0.5)
    allowed = (key_pos[None, :] >= query_start[:, None]) & (key_pos[None, :] <= query_pos[:, None])
    masked = jnp.where(allowed, scores, -jnp.inf)
    highest = jnp.max(masked, axis=-1, keepdims=True)
    weights = jnp.exp(masked - highest)
    totals = jnp.sum(weights, axis=-1)
    rounded = weights.astype(jnp.bfloat16)
    summed = jnp.einsum("gjqk,kgd->qgjd", rounded, value_three, preferred_element_type=jnp.float32)
    scaled = summed / jnp.transpose(totals, (2, 0, 1))[..., None]
    return scaled.reshape(query_block.shape[0], -1).astype(jnp.bfloat16)


def body(query_heads, key_heads, value_head_rows, out_weight, piece_lengths, block_order):
    num_ctx = lax.axis_size("ctx")
    ctx_index = lax.axis_index("ctx")
    tokens_dev = query_heads.shape[0]
    block_count = tokens_dev // BLK
    per_pair = block_count // num_ctx
    pair_table = block_order.reshape(num_ctx, num_ctx, per_pair)
    sent_ids = lax.dynamic_index_in_dim(pair_table, ctx_index, 1, keepdims=False)
    local_ids = sent_ids - ctx_index * block_count
    query_blocks = query_heads.reshape(block_count, BLK, -1)
    offsets = jnp.arange(BLK, dtype=jnp.int32)
    window_offsets = jnp.arange(MOST + BLK, dtype=jnp.int32)
    outgoing = jnp.take(query_blocks, local_ids, axis=0)
    arrived = lax.all_to_all(outgoing, "ctx", split_axis=0, concat_axis=0, tiled=True).reshape(
        block_count, BLK, -1
    )
    every_key, every_value = (
        lax.all_gather(key_heads, "ctx", axis=0, tiled=True),
        lax.all_gather(value_head_rows, "ctx", axis=0, tiled=True),
    )
    zero_rows = jnp.zeros((MOST, key_heads.shape[1]), jnp.bfloat16)
    key_padded = jnp.concatenate([zero_rows, every_key], axis=0)
    value_padded = jnp.concatenate([zero_rows, every_value], axis=0)
    owned_ids = lax.dynamic_slice_in_dim(block_order, ctx_index * block_count, block_count, 0)

    def attend_owned(item):
        query_block, block_id = item
        first_row = block_id * BLK
        key_window = lax.dynamic_slice_in_dim(key_padded, first_row, MOST + BLK, 0)
        value_window = lax.dynamic_slice_in_dim(value_padded, first_row, MOST + BLK, 0)
        query_pos = first_row + offsets
        key_pos = first_row - MOST + window_offsets
        return attend(
            query_block,
            key_window,
            value_window,
            query_pos,
            key_pos,
            piece_starts(query_pos, piece_lengths),
        )

    attention = lax.map(attend_owned, (arrived, owned_ids)).reshape(tokens_dev, -1)
    return lax.psum_scatter(
        jnp.dot(attention, out_weight, preferred_element_type=jnp.float32).astype(jnp.bfloat16),
        "kvh",
        scatter_dimension=0,
        tiled=True,
    )


def solution(mesh):
    placed = (P("ctx", "kvh"), P("ctx", "kvh"), P("ctx", "kvh"), P("kvh", None), P(), P())
    return jax.shard_map(
        body, mesh=mesh, in_specs=placed, out_specs=P(("ctx", "kvh"), None), check_vma=False
    )
```

profile of v0, /device:TPU:0, one launch (start us, length us, event | category | flops | bytes accessed | tf_op | source)
XLA Modules:
  0.0 1008.7 jit_solution(15170772434577554216)
XLA Ops:
  33.7 61.0 %all-gather.3.cloned.1.call-done = bf16[16384,256]{0,1:T(8,128)(2,1)} async-done(((bf16[2048,256]{0,1:T(8,128)(2,1)}), bf16[16384,256]{0,1:T(8,128)(2,1)}) %all-gather.3.cloned.1.call-update) | async-done | bytes 8388624 | tf_op jit(solution)/shard_map/all_gather | solution.py:55
  94.7 8.5 concatenate.6
  103.2 59.9 %all-gather.5.cloned.1.call-done = bf16[16384,256]{0,1:T(8,128)(2,1)} async-done(((bf16[2048,256]{0,1:T(8,128)(2,1)}), bf16[16384,256]{0,1:T(8,128)(2,1)}) %all-gather.5.cloned.1.call-update) | async-done | bytes 8388624 | tf_op jit(solution)/shard_map/all_gather | solution.py:54
  163.1 8.4 concatenate.7
  171.5 525.7 %while.13 = (s32[]{:T(128)}, bf16[16,128,1024]{2,1,0:T(8,128)(2,1)}, s32[16]{0:T(128)S(1)}, bf16[20480,256]{0,1:T(8,128)(2,1)}, s32[1,16]{1,0:T(1,128)S(1)}, /*i...) while((s32[]{:T(128)}, ...), condition=%wide.region_5.6_spmd.clone, body=%wide.region_1.5_spmd.clone.sunk | while | flops 2264064000 | bytes 69198160 | solution.py:78
  178.3 7.5 fusion.37
  185.8 9.4 fusion.38
  195.2 8.3 fusion.39
  211.2 7.5 fusion.37
  218.7 9.4 fusion.38
  228.1 8.3 fusion.39
  244.0 7.5 fusion.37
  251.5 9.4 fusion.38
  261.0 8.3 fusion.39
  276.9 7.5 fusion.37
  284.4 9.4 fusion.38
  293.8 8.3 fusion.39
  309.7 7.5 fusion.37
  317.3 9.4 fusion.38
  326.7 8.3 fusion.39
  342.6 7.5 fusion.37
  350.1 9.4 fusion.38
  359.5 8.3 fusion.39
  375.5 7.5 fusion.37
  383.0 9.4 fusion.38
  392.4 8.3 fusion.39
  408.3 7.5 fusion.37
  415.8 9.4 fusion.38
  425.3 8.3 fusion.39
  448.7 9.4 fusion.38
  458.1 8.3 fusion.39
  481.6 9.4 fusion.38
  491.0 8.3 fusion.39
  514.4 9.4 fusion.38
  523.8 8.3 fusion.39
  547.3 9.4 fusion.38
  556.7 8.3 fusion.39
  580.1 9.4 fusion.38
  589.5 8.3 fusion.39
  605.5 7.5 fusion.37
  613.0 9.4 fusion.38
  622.4 8.3 fusion.39
  645.9 9.4 fusion.38
  655.3 8.3 fusion.39
  678.7 9.4 fusion.38
  688.1 8.3 fusion.39
  697.3 24.2 %convolution_convert_fusion = bf16[2048,4096]{1,0:T(8,128)(2,1)} fusion(bf16[2048,1024]{1,0:T(8,128)(2,1)} %bitcast.89, bf16[1024,4096]{1,0:T(8,128)(2,1)} %param.11), kind=kOutput, calls=%fused_computation.23 | convolution fusion | flops 17188257792 | bytes 29360128 | tf_op jit(solution)/shard_map/dot_general | solution.py:80
  721.5 280.7 %reduce-scatter.2.cloned.1.call-done = bf16[512,4096]{1,0:T(8,128)(2,1)} async-done(((bf16[2048,4096]{1,0:T(8,128)(2,1)}), bf16[512,4096]{1,0:T(8,128)(2,1)}) %reduce-scatter.2.cloned.1.call-update) | async-done | bytes 4194320 | tf_op jit(solution)/shard_map/reduce_scatter | solution.py:79
  (180 shorter events, 191.9 us)
Async XLA Ops:
  6.5 4.7 copy-start.1
  6.5 88.2 %all-gather.3.cloned.1.call-start = ((), (), s32[]{:S(2)}) async-start(), calls=%async_computation.2 | async-start | bytes 9437184 | tf_op jit(solution)/shard_map/all_gather | solution.py:55
  8.9 154.2 %all-gather.5.cloned.1.call-start = ((), (), s32[]{:S(2)}) async-start(), calls=%async_computation.3 | async-start | bytes 9437184 | tf_op jit(solution)/shard_map/all_gather | solution.py:54
  28.0 5.5 copy-start
  28.0 143.6 %all-to-all-start = ((bf16[8,2,128,1024]{2,3,1,0:T(8,128)(2,1)}), bf16[8,2,128,1024]{2,3,1,0:T(8,128)(2,1)}, u32[]{:S(2)}, u32[]{:S(2)}) async-start(bf16[8,2,128,1024]{2,3,1,0:T(8,128)(2,1)} %broadcast_select_fusion), calls=%async_computation | async-start | bytes 8388608 | tf_op jit(solution)/shard_map/all_to_all | solution.py:50
  33.3 968.8 %reduce-scatter.2.cloned.1.call-start = ((), (), s32[]{:S(2)}) async-start(), calls=%async_computation.4 | async-start | bytes 20971520 | tf_op jit(solution)/shard_map/reduce_scatter | solution.py:79
Sparse Core Ops, SparseCore 0:
  9.2 85.4 all-gather.2
  96.6 66.4 all-gather.4
  721.6 280.4 reduce-scatter.1
where the time goes:
time: 1010 us
  waiting for transfers between devices  402 us (40%)
  matrix products  277 us (27%)
  other arithmetic  188 us (19%)
  local copies, waits for them, and re-layouts  113 us (11%)
  between operations  13.2 us (1%)
    reduce_scatter x1, waiting for transfers between devices, body(): lax.psum_scatter(jnp.dot(attention, out_weight, preferred_element_type=jn...  281 us
    reduce_sum x16, other arithmetic, attend(): totals = jnp.sum(weights, axis=-1)  151 us
    dot_general x16, matrix products, attend(): jnp.einsum('gjqk,kgd->qgjd', rounded, value_three, preferred_element_type...  133 us
    dot_general x16, matrix products, attend(): jnp.einsum('qgjd,kgd->gjqk', query_four, key_three, preferred_element_typ...  120 us
    all_gather x1, waiting for transfers between devices, body(): lax.all_gather(value_head_rows, 'ctx', axis=0, tiled=True)  61 us
    all_gather x1, waiting for transfers between devices, body(): lax.all_gather(key_heads, 'ctx', axis=0, tiled=True)  59.9 us
    dynamic_slice x16, local copies, waits for them, and re-layouts, attend_owned(): key_window = lax.dynamic_slice_in_dim(key_padded, first_row, MOST + BLK, 0)  40.9 us
    and x16, other arithmetic, attend(): (key_pos[None, :] >= query_start[:, None]) & (key_pos[None, :] <= query_p...  30.8 us
  transfers between devices with their start and end apart: 4, of which 3 were waited for; matrix products, arithmetic and copies ran while one was open for 4% of the time, Pallas kernels for 0%

commit v1 on v0

v1 whole, which is shorter than its diff:
```python
import functools
import math
import jax
import jax.numpy as jnp
from jax import lax
from jax.experimental import pallas as pl
from jax.experimental.pallas import tpu as pltpu
from jax.sharding import Mesh, PartitionSpec as P

HEAD_SIZE = 128
BLK = 128
CHUNK = 512
CTX = ("cg", "cp")
SCALE = math.log2(math.e) / HEAD_SIZE**0.5
NEG = -1e30


def attend_kernel(ids, lows, ends, lengths, q_ref, kv_ref, out_ref, q_four, top, acc):
    step = pl.program_id(0)
    heads = q_ref.shape[1] // HEAD_SIZE
    tokens = kv_ref.shape[0]
    first_row = ids[step] * BLK
    low = lows[step]
    for h in range(heads):
        q_four[h * BLK : (h + 1) * BLK, :] = q_ref[:, h * HEAD_SIZE : (h + 1) * HEAD_SIZE]
    top[...] = jnp.full_like(top, NEG)
    acc[...] = jnp.zeros_like(acc)
    query_pos = first_row + lax.broadcasted_iota(jnp.int32, (BLK, 1), 0)
    start = jnp.zeros((BLK, 1), jnp.int32)
    for p in range(ends.shape[0]):
        start = start + jnp.where(ends[p] <= query_pos, lengths[p], 0)
    count = (first_row + BLK - low + CHUNK - 1) // CHUNK

    def one(j, carry):
        begin = low + j * CHUNK
        at = pl.multiple_of(jnp.minimum(begin, tokens - CHUNK), BLK)
        key_pos = at + lax.broadcasted_iota(jnp.int32, (BLK, CHUNK), 1)
        allowed = (key_pos >= jnp.maximum(start, begin)) & (key_pos <= query_pos)
        bias = jnp.where(allowed, 0.0, NEG)
        keys = kv_ref[pl.ds(at, CHUNK), :HEAD_SIZE]
        values = kv_ref[pl.ds(at, CHUNK), HEAD_SIZE:]
        wide = jnp.concatenate([values, jnp.ones_like(values)], axis=1)
        for h in range(heads):
            rows = slice(h * BLK, (h + 1) * BLK)
            s = lax.dot_general(
                q_four[rows, :], keys, (((1,), (1,)), ((), ())), preferred_element_type=jnp.float32
            )
            s = s * SCALE + bias
            old = top[rows, :]
            new = jnp.maximum(old, jnp.max(s, axis=1, keepdims=True))
            top[rows, :] = new
            weights = jnp.exp2(s - new[:, :1]).astype(jnp.bfloat16)
            keep = jnp.exp2(old - new)
            keep = jnp.concatenate([keep, keep], axis=1)
            acc[rows, :] = acc[rows, :] * keep + jnp.dot(
                weights, wide, preferred_element_type=jnp.float32
            )
        return carry

    lax.fori_loop(0, count, one, 0)
    for h in range(heads):
        rows = slice(h * BLK, (h + 1) * BLK)
        out_ref[:, h * HEAD_SIZE : (h + 1) * HEAD_SIZE] = (
            acc[rows, :HEAD_SIZE] / acc[rows, HEAD_SIZE:]
        ).astype(jnp.bfloat16)


def attend(ids, lows, ends, lengths, query, kv):
    rows, width = query.shape
    tokens = kv.shape[0]
    stacked = BLK * width // HEAD_SIZE
    return pl.pallas_call(
        attend_kernel,
        out_shape=jax.ShapeDtypeStruct((rows, width), jnp.bfloat16),
        grid_spec=pltpu.PrefetchScalarGridSpec(
            num_scalar_prefetch=4,
            grid=(rows // BLK,),
            in_specs=[
                pl.BlockSpec((BLK, width), lambda i, *_: (i, 0)),
                pl.BlockSpec(memory_space=pltpu.VMEM),
            ],
            out_specs=pl.BlockSpec((BLK, width), lambda i, *_: (i, 0)),
            scratch_shapes=[
                pltpu.VMEM((stacked, HEAD_SIZE), jnp.bfloat16),
                pltpu.VMEM((stacked, HEAD_SIZE), jnp.float32),
                pltpu.VMEM((stacked, 2 * HEAD_SIZE), jnp.float32),
            ],
        ),
        compiler_params=pltpu.CompilerParams(vmem_limit_bytes=40 * 1024 * 1024),
        cost_estimate=pl.CostEstimate(
            flops=4 * rows * width * 1500, bytes_accessed=tokens * 512, transcendentals=rows * 4 * 1500
        ),
    )(ids, lows, ends, lengths, query, kv)


def body(query_heads, key_heads, value_head_rows, out_weight, piece_lengths, block_order):
    num_ctx = lax.axis_size(CTX)
    num_cg = lax.axis_size("cg")
    num_kvh = lax.axis_size("kvh")
    ctx_index = lax.axis_index(CTX)
    core = lax.axis_index("cp")
    tokens_dev = query_heads.shape[0]
    block_count = tokens_dev // BLK
    per_pair = block_count // num_ctx
    groups = key_heads.shape[1] // HEAD_SIZE
    width = query_heads.shape[1] // groups

    ends = jnp.cumsum(piece_lengths).astype(jnp.int32)
    owned = lax.dynamic_slice_in_dim(block_order, ctx_index * block_count, block_count, 0)
    first_rows = owned * BLK
    lows = jnp.sum(jnp.where(ends[None, :] <= first_rows[:, None], piece_lengths[None, :], 0), axis=1)
    lows = (lows // BLK * BLK).astype(jnp.int32)

    gathered_kv = []
    for g in range(groups):
        cols = slice(g * HEAD_SIZE, (g + 1) * HEAD_SIZE)
        pair = jnp.concatenate([key_heads[:, cols], value_head_rows[:, cols]], axis=1)
        if gathered_kv:
            pair, gathered_kv[-1] = lax.optimization_barrier((pair, gathered_kv[-1]))
        gathered_kv.append(lax.all_gather(pair, CTX, axis=0, tiled=True))

    pair_table = block_order.reshape(num_ctx, num_ctx, per_pair)
    sent_ids = lax.dynamic_index_in_dim(pair_table, ctx_index, 1, keepdims=False)
    local_ids = sent_ids - ctx_index * block_count
    outgoing = jnp.take(query_heads.reshape(block_count, BLK, -1), local_ids, axis=0)
    arrived = lax.all_to_all(outgoing, CTX, split_axis=0, concat_axis=0, tiled=True)
    arrived = arrived.reshape(tokens_dev, -1)

    half = out_weight.shape[1] // 2
    part = width // num_cg
    mine_w = lax.dynamic_slice_in_dim(out_weight, core * half, half, 1)
    weights = []
    last = gathered_kv[-1]
    for g in range(groups):
        piece = lax.dynamic_slice_in_dim(mine_w, g * width + lax.axis_index("cg") * part, part, 0)
        piece, last = lax.optimization_barrier((piece, last))
        weights.append(lax.all_gather(piece, ("kvh", "cg"), axis=0, tiled=True))
    gathered_kv[-1] = last

    swap = [(0, 1), (1, 0)]
    own, other = [], []
    for g in range(groups):
        attended = attend(
            owned, lows, ends, piece_lengths, arrived[:, g * width : (g + 1) * width], gathered_kv[g]
        )
        rows = lax.all_to_all(attended, "kvh", split_axis=0, concat_axis=1, tiled=True)
        own.append(rows)
        other.append(lax.ppermute(rows, "cp", swap))

    def project(parts):
        total = 0.0
        for x, w in zip(parts, weights):
            total = total + jnp.dot(x, w, preferred_element_type=jnp.float32)
        return total.astype(jnp.bfloat16)

    back = lax.ppermute(project(other), "cp", swap)
    here = project(own)
    return jnp.where(
        core == 0,
        jnp.concatenate([here, back], axis=1),
        jnp.concatenate([back, here], axis=1),
    )


def solution(mesh):
    num_ctx, num_kvh = mesh.devices.shape
    split = Mesh(mesh.devices.reshape(num_ctx // 2, 2, num_kvh), ("cg", "cp", "kvh"))
    placed = (P(CTX, "kvh"), P(CTX, "kvh"), P(CTX, "kvh"), P("kvh", None), P(), P())
    return jax.shard_map(
        body, mesh=split, in_specs=placed, out_specs=P(("cg", "cp", "kvh"), None), check_vma=False
    )
```

time: 1010 us -> 484 us (0.48)
  matrix products: 277 us -> 31.7 us
  other arithmetic: 188 us -> 10.3 us
  waiting for transfers between devices: 402 us -> 285 us
  Pallas kernels: 0 us -> 96.8 us
  local copies, waits for them, and re-layouts: 113 us -> 27.5 us
  starting transfers between devices: 5.43 us -> 19.4 us
    reduce_scatter x1 -> x0, waiting for transfers between devices: 281 us -> none  [body(): lax.psum_scatter(jnp.dot(attention, out_weight, preferred_element_type=jn...]
    dot_general x33 -> x4, matrix products: 277 us -> 31.7 us  [project(): total = total + jnp.dot(x, w, preferred_element_type=jnp.float32)]
    all_to_all x1 -> x3, waiting for transfers between devices: 0.01 us -> 175 us  [the longest x2 111 us: body(): lax.all_to_all(attended, 'kvh', split_axis=0, concat_axis=1, tiled=True)]
    reduce_sum x32 -> x1, other arithmetic: 152 us -> 0.18 us  [body(): jnp.sum(jnp.where(ends[None, :] <= first_rows[:, None], piece_lengths[Non...]
    pallas_call x0 -> x2, Pallas kernels: none -> 96.8 us  [attend(): pl.pallas_call(attend_kernel, out_shape=jax.ShapeDtypeStruct((rows, width...]
    dynamic_slice x49 -> x1, local copies, waits for them, and re-layouts: 66 us -> 2.8 us  [body(): lax.dynamic_slice_in_dim(mine_w, g * width + lax.axis_index('cg') * part,...]
    and x17 -> x1, other arithmetic: 30.8 us -> 0.01 us  [body(): jnp.take(query_heads.reshape(block_count, BLK, -1), local_ids, axis=0)]
    concatenate x2 -> x0, local copies, waits for them, and re-layouts: 16.9 us -> none  [the longest x1 8.52 us: body(): value_padded = jnp.concatenate([zero_rows, every_value], axis=0)]
  transfers between devices with their start and end apart: 4 -> 10, of which waited for: 3 -> 5; matrix products, arithmetic and copies ran while one was open for 4% -> 9% of each run, Pallas kernels for 0% -> 20%
where the time goes in v1:
time: 484 us; the launch traced here: 483 us
  waiting for transfers between devices  285 us (59%)
  Pallas kernels  96.8 us (20%)
  matrix products  31.7 us (7%)
  local copies, waits for them, and re-layouts  27.5 us (6%)
  starting transfers between devices  19.4 us (4%)
  between operations  13.3 us (3%)
  other arithmetic  10.3 us (2%)
    all_to_all x2, waiting for transfers between devices, body(): lax.all_to_all(attended, 'kvh', split_axis=0, concat_axis=1, tiled=True)  111 us
    all_gather x2, waiting for transfers between devices, body(): gathered_kv.append(lax.all_gather(pair, CTX, axis=0, tiled=True))  109 us
    pallas_call x2, Pallas kernels, attend(): pl.pallas_call(attend_kernel, out_shape=jax.ShapeDtypeStruct((rows, width...  96.8 us
    all_to_all x1, waiting for transfers between devices, body(): lax.all_to_all(outgoing, CTX, split_axis=0, concat_axis=0, tiled=True)  63.5 us
    dot_general x4, matrix products, project(): total = total + jnp.dot(x, w, preferred_element_type=jnp.float32)  31.7 us
  transfers between devices with their start and end apart: 10, of which 5 were waited for; matrix products, arithmetic and copies ran while one was open for 9% of the time, Pallas kernels for 20%

profile of v1, /device:TPU:0, one launch (start us, length us, event | category | flops | bytes accessed | tf_op | source)
XLA Modules:
  0.0 483.4 jit_solution(18249841780122529808)
XLA Ops:
  6.5 1.7 fusion.3
  8.2 1.1 pad_maximum_fusion.1
  9.3 0.0 all-gather.5.cloned.1.call-update
  9.3 0.0 all-gather.7.cloned.1.call-start
  9.4 1.1 pad_maximum_fusion
  10.5 56.0 %all-gather.5.cloned.1.call-done.kv_ref = bf16[16384,256]{1,0:T(8,128)(2,1)} async-done(((bf16[2048,256]{1,0:T(8,128)(2,1)}), bf16[16384,256]{1,0:T(8,128)(2,1)}) %all-gather.5.cloned.1.call-update) | async-done | bytes 8388624 | tf_op jit(solution)/shard_map/all_gather | solution.py:120
  66.5 0.0 all-gather.7.cloned.1.call-update
  66.5 0.0 all-gather.11.cloned.1.call-start
  66.6 2.8 fusion.1
  69.4 53.3 %all-gather.7.cloned.1.call-done.kv_ref = bf16[16384,256]{1,0:T(8,128)(2,1)} async-done(((bf16[2048,256]{1,0:T(8,128)(2,1)}), bf16[16384,256]{1,0:T(8,128)(2,1)}) %all-gather.7.cloned.1.call-update) | async-done | bytes 8388624 | tf_op jit(solution)/shard_map/all_gather | solution.py:120
  122.6 0.0 all-gather.11.cloned.1.call-update
  122.7 0.0 all-gather.9.cloned.1.call-start
  122.7 0.5 all-gather.9.cloned.1.call-update
  123.3 0.1 reshape.71
  123.4 0.1 copy.32
  123.5 0.1 copy.29
  123.6 0.1 reshape.76
  123.7 0.1 copy.28
  123.8 5.0 %gather_fusion = bf16[16,128,1024]{2,1,0:T(8,128)(2,1)} fusion(bf16[16,128,1024]{2,1,0:T(8,128)(2,1)} %bitcast.30, s32[1024]{0:T(1024)S(1)} %pad_clamp_fusion), kind=kCustom, calls=%fused_computation | custom fusion | bytes 8388672 | tf_op jit(solution)/shard_map/jit(_take)/gather | solution.py:125
  128.8 4.7 broadcast_select_fusion
  133.5 4.7 all-to-all-start
  138.2 0.1 copy.26
  138.3 0.1 reduce.ends
  138.4 0.1 broadcast_multiply_fusion
  138.5 0.2 select_reduce_fusion
  138.7 63.5 %all-to-all-done = bf16[8,2,128,1024]{3,2,1,0:T(8,128)(2,1)} async-done(((bf16[8,2,128,1024]{3,2,1,0:T(8,128)(2,1)}), bf16[8,2,128,1024]{3,2,1,0:T(8,128)(2,1)}, u32[]{:S(2)}, u32[]{:S(2)}) %all-to-all-start) | async-done | bytes 4194336 | tf_op jit(solution)/shard_map/all_to_all | solution.py:126
  202.2 4.3 fusion.2
  206.5 3.4 copy-done.3
  209.9 48.4 %shard_map.65 = bf16[2048,512]{1,0:T(8,128)(2,1)S(1)} custom-call(s32[16]{0:T(128)S(1)} %get-tuple-element.18.ids, s32[16]{0:T(128)S(1)} %fusion.lows, s32[16]{0:T(128)S(1)} %reduce.ends, s32[16]{0:T(128)S(1)} %copy-done.1, bf16[2048,512]{1,0:T(8,128)(2,1)S(1)} %get-tuple-element.22.q_ref, bf16[16384,256]{1,0:T(8,128)(2,1)S(1)} %copy-done.3), custom_call_target="tpu_custom_call" | custom-call | flops 6291456000 | bytes 8388608 | tf_op jit(solution)/shard_map/pallas_call | solution.py:72
  258.3 2.4 copy.31
  260.7 4.9 %all-to-all-start.2 = ((bf16[4,512,512]{1,2,0:T(8,128)(2,1)}), bf16[4,512,512]{1,2,0:T(8,128)(2,1)}, u32[]{:S(2)}, u32[]{:S(2)}) async-start(bf16[4,512,512]{1,2,0:T(8,128)(2,1)} %copy.31), calls=%async_computation.2 | async-start | bytes 4194304 | tf_op jit(solution)/shard_map/all_to_all | solution.py:146
  265.6 1.6 copy-done
  267.2 3.4 copy-done.2
  270.6 48.4 %shard_map.64 = bf16[2048,512]{1,0:T(8,128)(2,1)S(1)} custom-call(s32[16]{0:T(128)S(1)} %get-tuple-element.18.ids, s32[16]{0:T(128)S(1)} %fusion.lows, s32[16]{0:T(128)S(1)} %reduce.ends, s32[16]{0:T(128)S(1)} %copy-done.1, bf16[2048,512]{1,0:T(8,128)(2,1)S(1)} %copy-done, bf16[16384,256]{1,0:T(8,128)(2,1)S(1)} %copy-done.2), custom_call_target="tpu_custom_call" | custom-call | flops 6291456000 | bytes 8388608 | tf_op jit(solution)/shard_map/pallas_call | solution.py:72
  319.0 2.4 copy.30
  321.3 22.9 %all-to-all-done.2 = bf16[4,512,512]{1,2,0:T(8,128)(2,1)} async-done(((bf16[4,512,512]{1,2,0:T(8,128)(2,1)}), bf16[4,512,512]{1,2,0:T(8,128)(2,1)}, u32[]{:S(2)}, u32[]{:S(2)}) %all-to-all-start.2) | async-done | bytes 2097184 | tf_op jit(solution)/shard_map/all_to_all | solution.py:146
  344.2 3.8 all-to-all-start.1
  348.0 5.3 %collective-permute-start.1 = (bf16[512,2048]{0,1:T(8,128)(2,1)}, bf16[512,2048]{0,1:T(8,128)(2,1)}, u32[]{:S(2)}, u32[]{:S(2)}) collective-permute-start(bf16[512,2048]{0,1:T(8,128)(2,1)} %bitcast.11), channel_id=1, source_target_pairs={{0,4},{4,0},{1,5},{5,1},{2,6},{6,2},{3,7},{7,3},{8,12},{12,8},{9,1... | collective-permute-start | bytes 6291464 | tf_op jit(solution)/shard_map/ppermute | solution.py:148
  353.3 88.3 %all-to-all-done.1 = bf16[4,512,512]{1,2,0:T(8,128)(2,1)S(1)} async-done(((bf16[4,512,512]{1,2,0:T(8,128)(2,1)}), bf16[4,512,512]{1,2,0:T(8,128)(2,1)S(1)}, u32[]{:S(2)}, u32[]{:S(2)}) %all-to-all-start.1) | async-done | bytes 2097184 | tf_op jit(solution)/shard_map/all_to_all | solution.py:146
  441.6 0.6 collective-permute-start
  442.1 0.0 collective-permute-done.1
  442.2 10.6 %fusion.6 = f32[512,2048]{1,0:T(8,128)} fusion(bf16[512,2048]{0,1:T(8,128)(2,1)} %collective-permute-done.1, bf16[2048,2048]{1,0:T(8,128)(2,1)} %all-gather.11.cloned.1.call-done), kind=kOutput, calls=%fused_computation.24 | convolution fusion | flops 4294967296 | bytes 14680064 | tf_op jit(solution)/shard_map/dot_general | solution.py:153
  452.8 0.0 collective-permute-done
  452.8 9.9 %add_convert_fusion = bf16[512,2048]{1,0:T(8,128)(2,1)S(1)} fusion(f32[512,2048]{1,0:T(8,128)} %fusion.6, bf16[512,2048]{0,1:T(8,128)(2,1)} %collective-permute-done, bf16[2048,2048]{1,0:T(8,128)(2,1)} %all-gather.9.cloned.1.call-done), kind=kOutput, calls=%fused_computation.2 | convolution fusion | flops 4297064448 | bytes 16777216 | tf_op jit(solution)/shard_map/dot_general | solution.py:153
  462.7 0.1 collective-permute-start.2
  462.8 4.8 %fusion.5 = f32[512,2048]{1,0:T(8,128)S(1)} fusion(bf16[512,2048]{0,1:T(8,128)(2,1)S(1)} %bitcast.32, bf16[2048,2048]{1,0:T(8,128)(2,1)S(1)} %copy-done.6), kind=kOutput, calls=%fused_computation.23 | convolution fusion | flops 4294967296 | bytes 14680064 | tf_op jit(solution)/shard_map/dot_general | solution.py:153
  467.6 6.3 %add_convert_fusion.1 = bf16[512,2048]{1,0:T(8,128)(2,1)S(1)} fusion(f32[512,2048]{1,0:T(8,128)S(1)} %fusion.5, bf16[512,2048]{0,1:T(8,128)(2,1)} %bitcast.11, bf16[2048,2048]{1,0:T(8,128)(2,1)S(1)} %copy-done.5), kind=kOutput, calls=%fused_computation.3 | convolution fusion | flops 4297064448 | bytes 16777216 | tf_op jit(solution)/shard_map/dot_general | solution.py:153
  474.0 2.9 maximum_select_fusion
  (21 shorter events, 0.1 us)
Async XLA Ops:
  6.5 59.9 %all-gather.5.cloned.1.call-start = ((), (), s32[]{:S(2)}) async-start(), calls=%async_computation.3 | async-start | bytes 9437184 | tf_op jit(solution)/shard_map/all_gather | solution.py:120
  9.3 113.9 %copy-start.4 = (s32[128]{0:T(128)S(1)}, s32[128]{0:T(128)}, u32[]{:S(2)}) copy-start(s32[128]{0:T(128)} %param.11) | copy-start | bytes 1540
  9.3 113.3 %all-gather.7.cloned.1.call-start = ((), (), s32[]{:S(2)}) async-start(), calls=%async_computation.4 | async-start | bytes 9437184 | tf_op jit(solution)/shard_map/all_gather | solution.py:120
  66.5 375.7 %all-gather.11.cloned.1.call-start = ((), (), s32[]{:S(2)}) async-start(), calls=%async_computation.6 | async-start | bytes 8912896 | tf_op jit(solution)/shard_map/all_gather | solution.py:137
  122.7 330.1 %all-gather.9.cloned.1.call-start = ((), (), s32[]{:S(2)}) async-start(), calls=%async_computation.5 | async-start | bytes 8912896 | tf_op jit(solution)/shard_map/all_gather | solution.py:137
  133.5 4.7 copy-start.1
  133.5 68.7 %all-to-all-start = ((bf16[8,2,128,1024]{3,2,1,0:T(8,128)(2,1)}), bf16[8,2,128,1024]{3,2,1,0:T(8,128)(2,1)}, u32[]{:S(2)}, u32[]{:S(2)}) async-start(bf16[8,2,128,1024]{3,2,1,0:T(8,128)(2,1)} %broadcast_select_fusion), calls=%async_computation | async-start | bytes 8388608 | tf_op jit(solution)/shard_map/all_to_all | solution.py:126
  206.5 3.4 copy-start.3
  260.7 83.5 %all-to-all-start.2 = ((bf16[4,512,512]{1,2,0:T(8,128)(2,1)}), bf16[4,512,512]{1,2,0:T(8,128)(2,1)}, u32[]{:S(2)}, u32[]{:S(2)}) async-start(bf16[4,512,512]{1,2,0:T(8,128)(2,1)} %copy.31), calls=%async_computation.2 | async-start | bytes 4194304 | tf_op jit(solution)/shard_map/all_to_all | solution.py:146
  265.6 1.6 copy-start
  267.2 3.4 copy-start.2
  344.2 97.4 %all-to-all-start.1 = ((bf16[4,512,512]{1,2,0:T(8,128)(2,1)}), bf16[4,512,512]{1,2,0:T(8,128)(2,1)S(1)}, u32[]{:S(2)}, u32[]{:S(2)}) async-start(bf16[4,512,512]{1,2,0:T(8,128)(2,1)} %copy.30), calls=%async_computation.1 | async-start | bytes 4194304 | tf_op jit(solution)/shard_map/all_to_all | solution.py:146
  348.0 94.1 %collective-permute-start.1 = (bf16[512,2048]{0,1:T(8,128)(2,1)}, bf16[512,2048]{0,1:T(8,128)(2,1)}, u32[]{:S(2)}, u32[]{:S(2)}) collective-permute-start(bf16[512,2048]{0,1:T(8,128)(2,1)} %bitcast.11), channel_id=1, source_target_pairs={{0,4},{4,0},{1,5},{5,1},{2,6},{6,2},{3,7},{7,3},{8,12},{12,8},{9,1... | collective-permute-start | bytes 6291464 | tf_op jit(solution)/shard_map/ppermute | solution.py:148
  441.6 11.2 %collective-permute-start = (bf16[512,2048]{0,1:T(8,128)(2,1)S(1)}, bf16[512,2048]{0,1:T(8,128)(2,1)}, u32[]{:S(2)}, u32[]{:S(2)}) collective-permute-start(bf16[512,2048]{0,1:T(8,128)(2,1)S(1)} %bitcast.31), channel_id=1, source_target_pairs={{0,4},{4,0},{1,5},{5,1},{2,6},{6,2},{3,7},{7,3},{8,12},{12,8},{9,1... | collective-permute-start | bytes 6291464 | tf_op jit(solution)/shard_map/ppermute | solution.py:148
  452.8 10.0 %copy-start.6 = (bf16[2048,2048]{1,0:T(8,128)(2,1)S(1)}, bf16[2048,2048]{1,0:T(8,128)(2,1)}, u32[]{:S(2)}) copy-start(bf16[2048,2048]{1,0:T(8,128)(2,1)} %all-gather.9.cloned.1.call-done) | copy-start | bytes 25165828
  462.7 5.0 %copy-start.5 = (bf16[2048,2048]{1,0:T(8,128)(2,1)S(1)}, bf16[2048,2048]{1,0:T(8,128)(2,1)}, u32[]{:S(2)}) copy-start(bf16[2048,2048]{1,0:T(8,128)(2,1)} %all-gather.11.cloned.1.call-done) | copy-start | bytes 25165828
  462.7 11.3 %collective-permute-start.2 = (bf16[512,2048]{1,0:T(8,128)(2,1)S(1)}, bf16[512,2048]{1,0:T(8,128)(2,1)S(1)}, u32[]{:S(2)}, u32[]{:S(2)}) collective-permute-start(bf16[512,2048]{1,0:T(8,128)(2,1)S(1)} %add_convert_fusion), channel_id=1, source_target_pairs={{0,4},{4,0},{1,5},{5,1},{2,6},{6,2},{3,7},{7,3},{8,12},{12,8},{9,1... | collective-permute-start | bytes 6291464 | tf_op jit(solution)/shard_map/ppermute | solution.py:156
Sparse Core Ops, SparseCore 0:
  9.4 56.9 all-gather.4
  68.4 54.2 all-gather.6
  125.4 127.7 all-gather.10
  255.8 186.6 all-gather.8
